TPU v7x, 32 devices: a whole 2x2x4 slice. The times are simulated.
32 devices in a mesh: groups: 2 (over x), tm: 8 (over z, y), space: 2 (over core).
Axes of the slice: x: 2, y: 2, z: 4, core: 2. Of those that a mesh axis runs over, the one named last changes fastest.
Arguments:
- query_pre: bfloat16 [16, 8, 32, 2240], P(('groups', 'tm'), 'space'), parts along dimension 0, may hold values from -6 to 6
- key_pre: bfloat16 [16, 8, 32, 2240], P(('groups', 'tm'), 'space'), parts along dimension 0, may hold values from -6 to 6
- value_pre: bfloat16 [16, 8, 32, 2240], P(('groups', 'tm'), 'space'), parts along dimension 0, may hold values from -8 to 8
- grad_out: bfloat16 [16, 8, 32, 2240], P(('groups', 'tm'), 'space'), parts along dimension 0, may hold values from -96 to 96
- conv_taps: float32 [3, 3, 2240], replicated, may hold values from -4 to 4
Outputs:
- attended: bfloat16 [16, 8, 32, 2240], P(('groups', 'tm'), 'space'), parts along dimension 0
- query_grad: bfloat16 [16, 8, 32, 2240], P(('groups', 'tm'), 'space'), parts along dimension 0
- key_grad: bfloat16 [16, 8, 32, 2240], P(('groups', 'tm'), 'space'), parts along dimension 0
- value_grad: bfloat16 [16, 8, 32, 2240], P(('groups', 'tm'), 'space'), parts along dimension 0
- taps_grad: float32 [6, 3, 2240], P('groups'), parts along dimension 0
There are 2 independent parts, one for each index of `groups`. A program takes and returns all parts, laid end to end along the dimension named above; an argument that names none is the same for every part. Nothing has to cross between parts.
All inputs are finite; a program needn't handle non-finite values.
Results may differ from a plain program's by a relative error of at most 0.013.
Values may be sent and summed in bfloat16 or wider, within the bound.
A program may use at most 128 MiB of HBM per device.

v0:
```python
import jax
import jax.numpy as jnp
from jax import lax
from jax.sharding import PartitionSpec as P

HEADS = 20
HEAD_DIM = 112


def extended(block, sides, width):
    for axis, dim in sides:
        count = lax.axis_size(axis)
        forward = [(i, i + 1) for i in range(count - 1)]
        backward = [(target, source) for source, target in forward]
        low = lax.ppermute(
            lax.slice_in_dim(block, block.shape[dim] - width, None, axis=dim), axis, forward
        )
        high = lax.ppermute(lax.slice_in_dim(block, 0, width, axis=dim), axis, backward)
        block = jnp.concatenate([low, block, high], axis=dim)
    return block


def carried_in(part, axis, combine, identity):
    place = lax.axis_index(axis)
    gathered = jax.tree.map(lambda a: lax.all_gather(a, axis), part)
    state = jax.tree.map(lambda a, e: jnp.zeros_like(a) + jnp.asarray(e, a.dtype), part, identity)

    def one(turn, state):
        return combine(
            state, jax.tree.map(lambda a: lax.dynamic_index_in_dim(a, turn, 0, False), gathered)
        )

    return lax.fori_loop(0, place, one, state)


def carried_in_2(x, axis, join, neutral):
    count = lax.axis_size(axis)
    place = lax.axis_index(axis)
    ahead = count - 1 - place
    gathered = jax.tree.map(
        lambda a, kind: lax.all_gather(a.astype(kind), axis), x, (jnp.bfloat16, jnp.bfloat16)
    )
    state = jax.tree.map(lambda a, e: jnp.zeros_like(a) + jnp.asarray(e, a.dtype), x, neutral)

    def one(turn, state):
        source = count - 1 - turn
        return join(
            state,
            jax.tree.map(
                lambda a, own: lax.dynamic_index_in_dim(a, source, 0, False).astype(own.dtype),
                gathered,
                x,
            ),
        )

    return lax.fori_loop(0, ahead, one, state)


def mix_rows(padded, conv_taps, row_count, col_count, flipped):
    summed = jnp.zeros(padded.shape[:1] + (row_count, col_count, padded.shape[3]), jnp.float32)
    for row_off in range(3):
        for col_off in range(3):
            if flipped:
                window = padded[
                    :, 2 - row_off : 2 - row_off + row_count, 2 - col_off : 2 - col_off + col_count
                ]
            else:
                window = padded[:, row_off : row_off + row_count, col_off : col_off + col_count]
            summed = summed + conv_taps[row_off, col_off] * window
    return summed


def add_pair(earlier, later):
    return (earlier[0] + later[0], earlier[1] + later[1])


def shards(query_pre, key_pre, value_pre, grad_out, conv_taps):
    frame_count, row_count, col_count, model_width = value_pre.shape
    head_count = HEADS
    head_size = HEAD_DIM
    token_count = frame_count * row_count * col_count
    split = (token_count, head_count, head_size)
    highest = lax.Precision.HIGHEST
    value_rows, grad_band = (
        extended(value_pre, (("space", 1),), 1),
        extended(grad_out, (("space", 1),), 1),
    )
    value_pad = jnp.pad(value_rows, ((0, 0), (0, 0), (1, 1), (0, 0)))
    local = mix_rows(value_pad, conv_taps, row_count, col_count, False)
    queries = jnp.maximum(query_pre, 0).reshape(split)
    keys = jnp.maximum(key_pre, 0).reshape(split)
    values = value_pre.reshape(split)
    partial_value = jnp.einsum("the,thd->hed", keys, values, preferred_element_type=jnp.float32)
    key_sum = jnp.sum(keys, axis=0, dtype=jnp.float32)
    half_state, half_sum = (
        lax.psum_scatter(partial_value, "space", scatter_dimension=0, tiled=True),
        lax.psum_scatter(key_sum, "space", scatter_dimension=0, tiled=True),
    )
    before = carried_in(
        (half_state, half_sum),
        "tm",
        add_pair,
        (jnp.zeros_like(half_state), jnp.zeros_like(half_sum)),
    )
    kv_state, key_total = (
        lax.all_gather(before[0] + half_state, "space", axis=0, tiled=True),
        lax.all_gather(before[1] + half_sum, "space", axis=0, tiled=True),
    )
    query_f32 = queries.astype(jnp.float32)
    numerator = jnp.einsum("the,hed->thd", query_f32, kv_state, precision=highest)
    denominator = jnp.einsum("the,he->th", query_f32, key_total, precision=highest) + 1.0
    output_f32 = numerator / denominator[..., None]
    attended = (output_f32.reshape(value_pre.shape) + local).astype(jnp.bfloat16)
    cotangent = grad_out.astype(jnp.float32).reshape(split)
    grad_num = cotangent / denominator[..., None]
    grad_den = -jnp.sum(cotangent * output_f32, axis=-1) / denominator
    grad_query = (
        jnp.einsum("thd,hed->the", grad_num, kv_state, precision=highest)
        + grad_den[..., None] * key_total[None]
    )
    grad_partial = jnp.einsum("the,thd->hed", query_f32, grad_num, precision=highest)
    grad_keysum = jnp.einsum("th,the->he", grad_den, query_f32, precision=highest)
    half_grad, half_keysum = (
        lax.psum_scatter(grad_partial, "space", scatter_dimension=0, tiled=True),
        lax.psum_scatter(grad_keysum, "space", scatter_dimension=0, tiled=True),
    )
    after = carried_in_2(
        (half_grad, half_keysum),
        "tm",
        add_pair,
        (jnp.zeros_like(half_grad), jnp.zeros_like(half_keysum)),
    )
    grad_state, grad_total = (
        lax.all_gather(
            (after[0] + half_grad).astype(jnp.bfloat16), "space", axis=0, tiled=True
        ).astype(jnp.float32),
        lax.all_gather(
            (after[1] + half_keysum).astype(jnp.bfloat16), "space", axis=0, tiled=True
        ).astype(jnp.float32),
    )
    grad_key = (
        jnp.einsum("thd,hed->the", values.astype(jnp.float32), grad_state, precision=highest)
        + grad_total[None]
    )
    grad_mixed = jnp.einsum(
        "the,hed->thd", keys.astype(jnp.float32), grad_state, precision=highest
    ).reshape(value_pre.shape)
    query_grad = jnp.where(query_pre > 0, grad_query.reshape(value_pre.shape), 0.0).astype(
        jnp.bfloat16
    )
    key_grad = jnp.where(key_pre > 0, grad_key.reshape(value_pre.shape), 0.0).astype(jnp.bfloat16)
    grad_pad = jnp.pad(grad_band, ((0, 0), (0, 0), (1, 1), (0, 0)))
    value_grad = (grad_mixed + mix_rows(grad_pad, conv_taps, row_count, col_count, True)).astype(
        jnp.bfloat16
    )
    cotangent_full = grad_out.astype(jnp.float32)
    tap_rows = []
    for row_off in range(3):
        tap_cols = []
        for col_off in range(3):
            window = value_pad[:, row_off : row_off + row_count, col_off : col_off + col_count]
            tap_cols.append(jnp.sum(cotangent_full * window, axis=(0, 1, 2)))
        tap_rows.append(jnp.stack(tap_cols))
    taps_grad = lax.psum(jnp.stack(tap_rows), ("tm", "space"))
    return (attended, query_grad, key_grad, value_grad, taps_grad)


def solution(mesh):
    return jax.shard_map(
        shards,
        mesh=mesh,
        in_specs=(
            P(("groups", "tm"), "space", None, None),
            P(("groups", "tm"), "space", None, None),
            P(("groups", "tm"), "space", None, None),
            P(("groups", "tm"), "space", None, None),
            P(),
        ),
        out_specs=(
            P(("groups", "tm"), "space", None, None),
            P(("groups", "tm"), "space", None, None),
            P(("groups", "tm"), "space", None, None),
            P(("groups", "tm"), "space", None, None),
            P("groups", None, None),
        ),
        check_vma=False,
    )
```

profile of v0, /device:TPU:8, one launch (start us, length us, event | category | flops | bytes accessed | tf_op | source)
XLA Modules:
  0.0 254.5 jit_solution(9472925568814212947)
XLA Ops:
  13.3 10.1 %reduce-scatter.7.cloned.1.call-done = f32[10,112,112]{2,1,0:T(8,128)} async-done(((f32[20,112,112]{2,1,0:T(8,128)}), f32[10,112,112]{2,1,0:T(8,128)}) %reduce-scatter.7.cloned.1.call-update) | async-done | bytes 501776 | tf_op jit(solution)/shard_map/reduce_scatter | solution.py:96
  23.7 2.7 %fusion = f32[16,112]{1,0:T(8,128)S(1)} fusion(f32[20,112]{1,0:T(8,128)S(1)} %reduce_sum.102), kind=kCustom, calls=%all-reduce-scatter | all-reduce-scatter fusion | flops 3585 | bytes 16640
  26.4 2.2 collective-permute-start.4
  33.0 2.0 reshape.72
  35.7 28.8 %all-gather.4 = f32[8,10,112]{2,1,0:T(8,128)S(1)} all-gather(f32[1,10,112]{2,1,0:T(8,128)S(1)} %fusion.37), channel_id=3, replica_groups=mesh['groups'=2,'tm'=8,'space'=2] {'tm'}, dimensions={0}, use_global_device_ids=true | all-gather | bytes 40320 | tf_op jit(solution)/shard_map/all_gather | solution.py:25
  64.5 39.8 %all-gather.11.cloned.1.call-done = f32[80,112,112]{2,1,0:T(8,128)} async-done(((f32[10,112,112]{2,1,0:T(8,128)}), f32[80,112,112]{2,1,0:T(8,128)}) %all-gather.11.cloned.1.call-update) | async-done | bytes 4014096 | tf_op jit(solution)/shard_map/all_gather | solution.py:25
  104.3 2.5 while.26
  110.0 2.4 fusion.33
  112.5 13.9 %reduce-scatter.9.cloned.1.call-done = f32[10,112,112]{2,1,0:T(8,128)} async-done(((f32[20,112,112]{2,1,0:T(8,128)}), f32[10,112,112]{2,1,0:T(8,128)}) %reduce-scatter.9.cloned.1.call-update) | async-done | bytes 501776 | tf_op jit(solution)/shard_map/reduce_scatter | solution.py:124
  129.6 3.0 %collective-permute-start = (bf16[1,1,32,2240]{3,2,1,0:T(8,128)(2,1)S(1)}, bf16[1,1,32,2240]{3,2,1,0:T(8,128)(2,1)S(1)}, u32[]{:S(2)}, u32[]{:S(2)}) collective-permute-start(bf16[1,1,32,2240]{3,2,1,0:T(8,128)(2,1)S(1)} %get-tuple-element.171), channel_id=1, source_target_pairs={{0,1},{2,3},{4,5},{6,7},{8,9},{10,11},{12,13},{14,15},{16,17},{18,... | collective-permute-start | bytes 430088 | tf_op jit(solution)/shard_map/ppermute | solution.py:15
  134.7 3.7 %collective-permute-start.2 = (bf16[1,1,32,2240]{3,2,1,0:T(8,128)(2,1)}, bf16[1,1,32,2240]{3,2,1,0:T(8,128)(2,1)}, u32[]{:S(2)}, u32[]{:S(2)}) collective-permute-start(bf16[1,1,32,2240]{3,2,1,0:T(8,128)(2,1)} %get-tuple-element.169), channel_id=1, source_target_pairs={{0,1},{2,3},{4,5},{6,7},{8,9},{10,11},{12,13},{14,15},{16,17},{18,... | collective-permute-start | bytes 430088 | tf_op jit(solution)/shard_map/ppermute | solution.py:15
  145.5 2.9 %all_gather.40 = f32[20,112,112]{2,1,0:T(8,128)S(1)} all-gather(f32[10,112,112]{2,1,0:T(8,128)S(1)} %add.145), channel_id=1, replica_groups=mesh['groups'=2,'tm'=8,'space'=2] {'space'}, dimensions={0}, use_global_device_ids=true | all-gather | bytes 1505280 | tf_op jit(solution)/shard_map/all_gather | solution.py:106
  148.5 2.7 %multiply_reduce_fusion = (f32[128,20]{0,1:T(8,128)}, f32[128,20,112]{0,2,1:T(8,128)}) fusion(f32[128,20,112]{0,2,1:T(8,128)S(1)} %copy-done.18, f32[128,20]{0,1:T(8,128)S(1)} %copy-done.37, f32[20,112,112]{2,1,0:T(8,128)S(1)} %all_gather.40, bf16[128,20,112]{0,2,1:T(8,128)(2,1)S(1)} %copy-done.10), kind=kOutput, calls=%fused_computation.62 | convolution fusion | flops 386209280 | bytes 3891200 | tf_op jit(solution)/shard_map/the,hed->thd/dot_general | solution.py:110
  151.2 2.9 %copy.41 = f32[128,20,112]{2,1,0:T(8,128)} copy(f32[128,20,112]{0,2,1:T(8,128)} %get-tuple-element.174) | data formatting | bytes 2293760 | tf_op jit(solution)/shard_map/div | solution.py:112
  154.2 2.7 %reshape.73 = f32[1,4,32,2240]{3,2,1,0:T(8,128)} reshape(f32[128,20,112]{2,1,0:T(8,128)} %copy.41) | data formatting | bytes 2293760 | tf_op jit(solution)/shard_map/reshape | solution.py:113
  158.6 2.7 %fusion.1 = f32[16,112]{1,0:T(8,128)S(1)} fusion(f32[20,112]{1,0:T(8,128)S(1)} %bitcast.88), kind=kCustom, calls=%all-reduce-scatter.1 | all-reduce-scatter fusion | flops 3585 | bytes 16640
  161.3 2.2 collective-permute-start.5
  163.6 3.3 %fusion.15 = bf16[1,4,32,2240]{3,2,1,0:T(8,128)(2,1)} fusion(f32[1,4,32,2240]{3,2,1,0:T(8,128)} %reshape.73, bf16[1,4,32,2240]{3,2,1,0:T(8,128)(2,1)S(1)} %copy-done, bf16[1,1,32,2240]{3,2,1,0:T(8,128)(2,1)S(1)} %collective-permute-done.1, bf16[1,1,32,2240]{3,2,1,0:T(8,128)(2,1)} %copy-done.14, f32[2240]{0:T(1024)} %get-tuple-element.143, ...), kind=kLoop, calls=%fused_computation.42 | loop fusion | flops 8601600 | bytes 6101760 | tf_op jit(solution)/shard_map/convert_element_type | solution.py:113
  170.3 28.0 %all-gather.6 = bf16[8,10,112]{2,1,0:T(8,128)(2,1)S(1)} all-gather(bf16[1,10,112]{2,1,0:T(8,128)(2,1)S(1)} %fusion.39), channel_id=5, replica_groups=mesh['groups'=2,'tm'=8,'space'=2] {'tm'}, dimensions={0}, use_global_device_ids=true | all-gather | bytes 20160 | tf_op jit(solution)/shard_map/all_gather | solution.py:41
  198.4 5.6 %while.27 = (s32[]{:T(128)}, f32[10,112,112]{2,1,0:T(8,128)S(1)}, f32[10,112]{1,0:T(8,128)S(1)}, s32[]{:T(128)}, bf16[8,10,112,112]{3,2,1,0:T(8,128)(2,1)}, /*in...) while((s32[]{:T(128)}, f32[10,112,112]{2,1,0:T(8,128)S(1)}, ...), condition=%wide.region_9.10_spmd, body=%wide.region_8.9_spmd.sunk | while | flops 253126 | bytes 1265763 | solution.py:56
  204.1 2.3 all_gather.46
  217.7 2.8 %select_convert_fusion = (bf16[1,4,32,2240]{3,2,1,0:T(8,128)(2,1)}, bf16[1,4,32,2240]{3,2,1,0:T(8,128)(2,1)}) fusion(bf16[1,4,32,2240]{3,2,1,0:T(8,128)(2,1)} %reshape.76, bf16[1,4,32,2240]{3,2,1,0:T(8,128)(2,1)S(1)} %copy-done.4, bf16[1,4,32,2240]{3,2,1,0:T(8,128)(2,1)} %reshape.75, bf16[1,4,32,2240]{3,2,1,0:T(8,128)(2,1)} %param.9), kind=kLoop, calls=%fused_computation.59 | loop fusion | flops 2007040 | bytes 3440640 | tf_op jit(solution)/shard_map/convert_element_type | solution.py:151
  220.6 2.7 %fusion.22 = bf16[1,4,32,2240]{3,2,1,0:T(8,128)(2,1)} fusion(f32[1,4,32,2240]{3,2,1,0:T(8,128)S(1)} %reshape.77, bf16[1,4,32,2240]{3,2,1,0:T(8,128)(2,1)S(1)} %copy-done.2, bf16[1,6,34,2240]{3,2,1,0:T(8,128)(2,1)S(1)} %select_maximum_fusion, bf16[1,1,32,2240]{3,2,1,0:T(8,128)(2,1)} %collective-permute-done.2, bf16[1,1,32,2240]{3,2,1,0:T(8,128)(2,1)S(1)} %copy-done.21, ...), kind=kLoop, calls=%fused_computation.49 | loop fusion | flops 8601600 | bytes 6101760 | tf_op jit(solution)/shard_map/convert_element_type | solution.py:153
  223.3 22.5 %all-reduce.8.cloned.1.call-done = f32[3,3,2240]{2,1,0:T(4,128)} async-done(((f32[3,3,2240]{2,1,0:T(4,128)}), f32[3,3,2240]{2,1,0:T(4,128)}) %all-reduce.8.cloned.1.call-update) | async-done | bytes 80656 | tf_op jit(solution)/shard_map/psum | solution.py:164
  (179 shorter events, 51.2 us)
Async XLA Ops:
  8.0 15.4 %reduce-scatter.7.cloned.1.call-start = ((), (), s32[]{:S(2)}) async-start(), calls=%async_computation.2 | async-start | bytes 1720320 | tf_op jit(solution)/shard_map/reduce_scatter | solution.py:96
  13.3 10.3 %copy-start.3 = (bf16[1,4,32,2240]{3,2,1,0:T(8,128)(2,1)S(1)}, bf16[1,4,32,2240]{3,2,1,0:T(8,128)(2,1)}, u32[]{:S(2)}) copy-start(bf16[1,4,32,2240]{3,2,1,0:T(8,128)(2,1)} %param.10) | copy-start | bytes 1720324
  13.3 15.4 %copy-start.12 = (bf16[1,4,32,2240]{3,2,1,0:T(8,128)(2,1)S(1)}, bf16[1,4,32,2240]{3,2,1,0:T(8,128)(2,1)}, u32[]{:S(2)}) copy-start(bf16[1,4,32,2240]{3,2,1,0:T(8,128)(2,1)} %param.9) | copy-start | bytes 1720324
  13.3 91.0 %all-gather.11.cloned.1.call-start = ((), (), s32[]{:S(2)}) async-start(), calls=%async_computation.5 | async-start | bytes 5160960 | tf_op jit(solution)/shard_map/all_gather | solution.py:25
  23.4 6.1 %copy-start.1 = (bf16[1,4,32,2240]{3,2,1,0:T(8,128)(2,1)S(1)}, bf16[1,4,32,2240]{3,2,1,0:T(8,128)(2,1)}, u32[]{:S(2)}) copy-start(bf16[1,4,32,2240]{3,2,1,0:T(8,128)(2,1)} %param.12) | copy-start | bytes 1720324
  23.5 102.9 %reduce-scatter.9.cloned.1.call-start = ((), (), s32[]{:S(2)}) async-start(), calls=%async_computation.3 | async-start | bytes 1720320 | tf_op jit(solution)/shard_map/reduce_scatter | solution.py:124
  26.4 9.1 %collective-permute-start.4 = (f32[6,112]{1,0:T(8,128)S(1)}, f32[6,112]{1,0:T(8,128)S(1)}, u32[]{:S(2)}, u32[]{:S(2)}) collective-permute-start(f32[6,112]{1,0:T(8,128)S(1)} %slice.158), channel_id=1, source_target_pairs={{0,1},{2,3},{4,5},{6,7},{8,9},{10,11},{12,13},{14,15},{16,17},{18,... | collective-permute-start | bytes 8072
  35.5 74.5 %copy-start.9 = (bf16[128,20,112]{0,2,1:T(8,128)(2,1)}, bf16[128,20,112]{0,2,1:T(8,128)(2,1)S(1)}, u32[]{:S(2)}) copy-start(bf16[128,20,112]{0,2,1:T(8,128)(2,1)S(1)} %copy.40) | copy-start | bytes 1720324
  35.7 68.6 %copy-start.31 = (f32[22,112]{1,0:T(8,128)}, f32[22,112]{1,0:T(8,128)S(1)}, u32[]{:S(2)}) copy-start(f32[22,112]{1,0:T(8,128)S(1)} %concatenate.24) | copy-start | bytes 29572
  104.3 5.7 %copy-start.17 = (f32[128,20,112]{0,2,1:T(8,128)S(1)}, f32[128,20,112]{0,2,1:T(8,128)}, u32[]{:S(2)}) copy-start(f32[128,20,112]{0,2,1:T(8,128)} %copy.42) | copy-start | bytes 3440644
  112.4 26.0 %copy-start.32 = (f32[3,3,2240]{2,1,0:T(4,128)S(1)}, f32[3,3,2240]{2,1,0:T(4,128)}, u32[]{:S(2)}) copy-start(f32[3,3,2240]{2,1,0:T(4,128)} %param.13) | copy-start | bytes 241924
  112.4 85.9 %all-gather.13.cloned.1.call-start = ((), (), s32[]{:S(2)}) async-start(), calls=%async_computation.6 | async-start | bytes 2580480 | tf_op jit(solution)/shard_map/all_gather | solution.py:41
  128.2 117.6 %all-reduce.8.cloned.1.call-start = ((), (), s32[]{:S(2)}) async-start(), calls=%async_computation.4 | async-start | bytes 221184 | tf_op jit(solution)/shard_map/psum | solution.py:164
  128.3 10.9 %collective-permute-start.1 = (bf16[1,1,32,2240]{3,2,1,0:T(8,128)(2,1)S(1)}, bf16[1,1,32,2240]{3,2,1,0:T(8,128)(2,1)S(1)}, u32[]{:S(2)}, u32[]{:S(2)}) collective-permute-start(bf16[1,1,32,2240]{3,2,1,0:T(8,128)(2,1)S(1)} %get-tuple-element.172), channel_id=1, source_target_pairs={{1,0},{3,2},{5,4},{7,6},{9,8},{11,10},{13,12},{15,14},{17,16},{19,... | collective-permute-start | bytes 430088 | tf_op jit(solution)/shard_map/ppermute | solution.py:18
  129.6 9.6 %collective-permute-start = (bf16[1,1,32,2240]{3,2,1,0:T(8,128)(2,1)S(1)}, bf16[1,1,32,2240]{3,2,1,0:T(8,128)(2,1)S(1)}, u32[]{:S(2)}, u32[]{:S(2)}) collective-permute-start(bf16[1,1,32,2240]{3,2,1,0:T(8,128)(2,1)S(1)} %get-tuple-element.171), channel_id=1, source_target_pairs={{0,1},{2,3},{4,5},{6,7},{8,9},{10,11},{12,13},{14,15},{16,17},{18,... | collective-permute-start | bytes 430088 | tf_op jit(solution)/shard_map/ppermute | solution.py:15
  133.4 8.2 %collective-permute-start.3 = (bf16[1,1,32,2240]{3,2,1,0:T(8,128)(2,1)}, bf16[1,1,32,2240]{3,2,1,0:T(8,128)(2,1)S(1)}, u32[]{:S(2)}, u32[]{:S(2)}) collective-permute-start(bf16[1,1,32,2240]{3,2,1,0:T(8,128)(2,1)} %get-tuple-element.170), channel_id=1, source_target_pairs={{1,0},{3,2},{5,4},{7,6},{9,8},{11,10},{13,12},{15,14},{17,16},{19,... | collective-permute-start | bytes 430088 | tf_op jit(solution)/shard_map/ppermute | solution.py:18
  134.7 7.6 %collective-permute-start.2 = (bf16[1,1,32,2240]{3,2,1,0:T(8,128)(2,1)}, bf16[1,1,32,2240]{3,2,1,0:T(8,128)(2,1)}, u32[]{:S(2)}, u32[]{:S(2)}) collective-permute-start(bf16[1,1,32,2240]{3,2,1,0:T(8,128)(2,1)} %get-tuple-element.169), channel_id=1, source_target_pairs={{0,1},{2,3},{4,5},{6,7},{8,9},{10,11},{12,13},{14,15},{16,17},{18,... | collective-permute-start | bytes 430088 | tf_op jit(solution)/shard_map/ppermute | solution.py:15
  144.4 4.1 %copy-start.37 = (f32[128,20]{0,1:T(8,128)S(1)}, f32[128,20]{0,1:T(8,128)}, u32[]{:S(2)}) copy-start(f32[128,20]{0,1:T(8,128)} %copy-done.36) | copy-start | bytes 30724
  154.1 9.4 %copy-start.22 = (f32[2240]{0:T(1024)S(1)}, f32[2240]{0:T(1024)}, u32[]{:S(2)}) copy-start(f32[2240]{0:T(1024)} %get-tuple-element.137) | copy-start | bytes 26884
  161.3 8.9 %collective-permute-start.5 = (f32[6,112]{1,0:T(8,128)S(1)}, f32[6,112]{1,0:T(8,128)S(1)}, u32[]{:S(2)}, u32[]{:S(2)}) collective-permute-start(f32[6,112]{1,0:T(8,128)S(1)} %slice.159), channel_id=1, source_target_pairs={{0,1},{2,3},{4,5},{6,7},{8,9},{10,11},{12,13},{14,15},{16,17},{18,... | collective-permute-start | bytes 8072
  163.5 3.4 %copy-start.16 = (f32[20,112,112]{2,1,0:T(8,128)S(1)}, f32[20,112,112]{2,1,0:T(8,128)}, u32[]{:S(2)}) copy-start(f32[20,112,112]{2,1,0:T(8,128)} %copy-done.15) | copy-start | bytes 3010564
  163.5 3.4 %copy-start.19 = (f32[128,20,112]{0,2,1:T(8,128)S(1)}, f32[128,20,112]{0,2,1:T(8,128)}, u32[]{:S(2)}) copy-start(f32[128,20,112]{0,2,1:T(8,128)} %copy.42) | copy-start | bytes 3440644
  198.4 5.6 %copy-start.13 = (f32[10,112,112]{2,1,0:T(8,128)S(1)}, f32[10,112,112]{2,1,0:T(8,128)}, u32[]{:S(2)}) copy-start(f32[10,112,112]{2,1,0:T(8,128)} %reduce-scatter.9.cloned.1.call-done) | copy-start | bytes 1505284
  204.0 4.4 %copy-start.6 = (bf16[128,20,112]{0,2,1:T(8,128)(2,1)S(1)}, bf16[128,20,112]{0,2,1:T(8,128)(2,1)}, u32[]{:S(2)}) copy-start(bf16[128,20,112]{0,2,1:T(8,128)(2,1)} %copy-done.5) | copy-start | bytes 1720324
  (27 other events, 66.7 us)
Sparse Core Ops, SparseCore 0:
  13.4 9.9 reduce-scatter.6
  25.6 78.6 all-gather.10
  112.5 13.7 reduce-scatter.8
  128.4 52.3 all-gather.12
Sparse Core Ops, SparseCore 1:
  141.7 104.1 all-reduce.7
where the time goes:
time: 256 us; the launch traced here: 255 us
  waiting for transfers between devices  86.4 us (34%)
  blocking collectives  71.2 us (28%)
  other arithmetic  27.1 us (11%)
  local copies, waits for them, and re-layouts  26.9 us (11%)
  between operations  16.6 us (6%)
  starting transfers between devices  14 us (5%)
  matrix products  12.1 us (5%)
    all_gather x1, waiting for transfers between devices, carried_in(): gathered = jax.tree.map(lambda a: lax.all_gather(a, axis), part)  39.8 us
    all_gather x1, blocking collectives, carried_in(): gathered = jax.tree.map(lambda a: lax.all_gather(a, axis), part)  28.8 us
    all_gather x1, blocking collectives, carried_in_2(): lax.all_gather(a.astype(kind), axis)  28 us
    psum x1, waiting for transfers between devices, shards(): taps_grad = lax.psum(jnp.stack(tap_rows), ('tm', 'space'))  22.5 us
    reduce_scatter x1, waiting for transfers between devices, shards(): lax.psum_scatter(grad_partial, 'space', scatter_dimension=0, tiled=True)  13.9 us
    reduce_scatter x1, waiting for transfers between devices, shards(): lax.psum_scatter(partial_value, 'space', scatter_dimension=0, tiled=True)  10.1 us
    add x14, other arithmetic, add_pair(): return (earlier[0] + later[0], earlier[1] + later[1])  7.9 us
    ppermute x2, starting transfers between devices, extended(): lax.ppermute(lax.slice_in_dim(block, block.shape[dim] - width, None, axis...  6.74 us
  transfers between devices with their start and end apart: 11, of which 4 were waited for; matrix products, arithmetic and copies ran while one was open for 22% of the time, Pallas kernels for 0%

commit v1 on v0

--- a/solution.py
+++ b/solution.py
@@ -161,7 +161,7 @@
             window = value_pad[:, row_off : row_off + row_count, col_off : col_off + col_count]
             tap_cols.append(jnp.sum(cotangent_full * window, axis=(0, 1, 2)))
         tap_rows.append(jnp.stack(tap_cols))
-    taps_grad = lax.psum(jnp.stack(tap_rows), ("tm", "space"))
+    taps_grad = lax.psum(lax.psum(jnp.stack(tap_rows), "space"), "tm")
     return (attended, query_grad, key_grad, value_grad, taps_grad)
 
 

time: 256 us -> 285 us (1.11)
  waiting for transfers between devices: 86.4 us -> 115 us
    psum x1 -> x2, waiting for transfers between devices: 22.5 us -> 58.1 us  [shards(): taps_grad = lax.psum(lax.psum(jnp.stack(tap_rows), 'space'), 'tm')]
    reduce_scatter x1, waiting for transfers between devices: 13.9 us -> 6.04 us  [shards(): lax.psum_scatter(grad_partial, 'space', scatter_dimension=0, tiled=True)]
  transfers between devices with their start and end apart: 11 -> 12, of which waited for: 4 -> 6; matrix products, arithmetic and copies ran while one was open for 22% -> 20% of each run, Pallas kernels for 0% -> 0%
where the time goes in v1:
time: 285 us; the launch traced here: 283 us
  waiting for transfers between devices  115 us (40%)
  blocking collectives  71.6 us (25%)
  local copies, waits for them, and re-layouts  27.5 us (10%)
  other arithmetic  25.7 us (9%)
  between operations  15.5 us (5%)
  starting transfers between devices  14 us (5%)
  matrix products  13.4 us (5%)
    psum x2, waiting for transfers between devices, shards(): taps_grad = lax.psum(lax.psum(jnp.stack(tap_rows), 'space'), 'tm')  58.1 us
    all_gather x1, waiting for transfers between devices, carried_in(): gathered = jax.tree.map(lambda a: lax.all_gather(a, axis), part)  39.8 us
    all_gather x1, blocking collectives, carried_in(): gathered = jax.tree.map(lambda a: lax.all_gather(a, axis), part)  28.8 us
    all_gather x1, blocking collectives, carried_in_2(): lax.all_gather(a.astype(kind), axis)  28.4 us
    reduce_scatter x1, waiting for transfers between devices, shards(): lax.psum_scatter(partial_value, 'space', scatter_dimension=0, tiled=True)  10.1 us
    add x14, other arithmetic, add_pair(): return (earlier[0] + later[0], earlier[1] + later[1])  7.81 us
    ppermute x2, starting transfers between devices, extended(): lax.ppermute(lax.slice_in_dim(block, block.shape[dim] - width, None, axis...  6.74 us
    reduce_scatter x1, waiting for transfers between devices, shards(): lax.psum_scatter(grad_partial, 'space', scatter_dimension=0, tiled=True)  6.04 us
  transfers between devices with their start and end apart: 12, of which 6 were waited for; matrix products, arithmetic and copies ran while one was open for 20% of the time, Pallas kernels for 0%

profile of v1, /device:TPU:8, one launch (start us, length us, event | category | flops | bytes accessed | tf_op | source)
XLA Modules:
  0.0 283.0 jit_solution(12367902203266790285)
XLA Ops:
  13.3 10.1 %reduce-scatter.7.cloned.1.call-done = f32[10,112,112]{2,1,0:T(8,128)} async-done(((f32[20,112,112]{2,1,0:T(8,128)}), f32[10,112,112]{2,1,0:T(8,128)}) %reduce-scatter.7.cloned.1.call-update) | async-done | bytes 501776 | tf_op jit(solution)/shard_map/reduce_scatter | solution.py:96
  23.7 2.7 fusion
  26.4 2.2 collective-permute-start.4
  35.7 28.8 %all-gather.4 = f32[8,10,112]{2,1,0:T(8,128)S(1)} all-gather(f32[1,10,112]{2,1,0:T(8,128)S(1)} %fusion.37), channel_id=3, replica_groups=mesh['groups'=2,'tm'=8,'space'=2] {'tm'}, dimensions={0}, use_global_device_ids=true | all-gather | bytes 40320 | tf_op jit(solution)/shard_map/all_gather | solution.py:25
  64.5 39.8 %all-gather.11.cloned.1.call-done = f32[80,112,112]{2,1,0:T(8,128)} async-done(((f32[10,112,112]{2,1,0:T(8,128)}), f32[80,112,112]{2,1,0:T(8,128)}) %all-gather.11.cloned.1.call-update) | async-done | bytes 4014096 | tf_op jit(solution)/shard_map/all_gather | solution.py:25
  104.3 2.4 while.26
  109.2 3.6 %fusion.33 = f32[20,112,112]{2,1,0:T(8,128)} fusion(bf16[128,20,112]{0,2,1:T(8,128)(2,1)S(1)} %copy.40, f32[128,20,112]{0,2,1:T(8,128)} %copy.42, f32[128,20]{0,1:T(8,128)S(1)} %fusion.34), kind=kOutput, calls=%fused_computation.74 | convolution fusion | flops 385638400 | bytes 2734080 | tf_op jit(solution)/shard_map/the,thd->hed/dot_general | solution.py:121
  114.2 3.0 %collective-permute-start = (bf16[1,1,32,2240]{3,2,1,0:T(8,128)(2,1)S(1)}, bf16[1,1,32,2240]{3,2,1,0:T(8,128)(2,1)S(1)}, u32[]{:S(2)}, u32[]{:S(2)}) collective-permute-start(bf16[1,1,32,2240]{3,2,1,0:T(8,128)(2,1)S(1)} %get-tuple-element.171), channel_id=1, source_target_pairs={{0,1},{2,3},{4,5},{6,7},{8,9},{10,11},{12,13},{14,15},{16,17},{18,... | collective-permute-start | bytes 430088 | tf_op jit(solution)/shard_map/ppermute | solution.py:15
  120.7 6.0 %reduce-scatter.9.cloned.1.call-done = f32[10,112,112]{2,1,0:T(8,128)} async-done(((f32[20,112,112]{2,1,0:T(8,128)}), f32[10,112,112]{2,1,0:T(8,128)}) %reduce-scatter.9.cloned.1.call-update) | async-done | bytes 501776 | tf_op jit(solution)/shard_map/reduce_scatter | solution.py:124
  130.0 3.7 %collective-permute-start.2 = (bf16[1,1,32,2240]{3,2,1,0:T(8,128)(2,1)S(1)}, bf16[1,1,32,2240]{3,2,1,0:T(8,128)(2,1)}, u32[]{:S(2)}, u32[]{:S(2)}) collective-permute-start(bf16[1,1,32,2240]{3,2,1,0:T(8,128)(2,1)S(1)} %get-tuple-element.169), channel_id=1, source_target_pairs={{0,1},{2,3},{4,5},{6,7},{8,9},{10,11},{12,13},{14,15},{16,17},{18,... | collective-permute-start | bytes 430088 | tf_op jit(solution)/shard_map/ppermute | solution.py:15
  136.7 11.9 %all-reduce.9.cloned.1.call-done = f32[3,3,2240]{2,1,0:T(4,128)} async-done(((f32[3,3,2240]{2,1,0:T(4,128)}), f32[3,3,2240]{2,1,0:T(4,128)}) %all-reduce.9.cloned.1.call-update) | async-done | bytes 80656 | tf_op jit(solution)/shard_map/psum | solution.py:164
  150.4 2.9 %all_gather.40 = f32[20,112,112]{2,1,0:T(8,128)S(1)} all-gather(f32[10,112,112]{2,1,0:T(8,128)S(1)} %add.147), channel_id=1, replica_groups=mesh['groups'=2,'tm'=8,'space'=2] {'space'}, dimensions={0}, use_global_device_ids=true | all-gather | bytes 1505280 | tf_op jit(solution)/shard_map/all_gather | solution.py:106
  153.4 2.7 multiply_reduce_fusion
  156.1 2.9 %copy.41 = f32[128,20,112]{2,1,0:T(8,128)} copy(f32[128,20,112]{0,2,1:T(8,128)} %get-tuple-element.174) | data formatting | bytes 2293760 | tf_op jit(solution)/shard_map/div | solution.py:112
  159.0 2.8 reshape.73
  163.5 2.8 fusion.1
  166.3 2.2 collective-permute-start.5
  168.5 3.3 %fusion.15 = bf16[1,4,32,2240]{3,2,1,0:T(8,128)(2,1)} fusion(f32[1,4,32,2240]{3,2,1,0:T(8,128)} %reshape.73, bf16[1,4,32,2240]{3,2,1,0:T(8,128)(2,1)S(1)} %copy-done, bf16[1,1,32,2240]{3,2,1,0:T(8,128)(2,1)S(1)} %collective-permute-done.1, bf16[1,1,32,2240]{3,2,1,0:T(8,128)(2,1)} %copy-done.13, f32[2240]{0:T(1024)} %get-tuple-element.143, ...), kind=kLoop, calls=%fused_computation.42 | loop fusion | flops 8601600 | bytes 6101760 | tf_op jit(solution)/shard_map/convert_element_type | solution.py:113
  175.3 28.4 %all-gather.6 = bf16[8,10,112]{2,1,0:T(8,128)(2,1)S(1)} all-gather(bf16[1,10,112]{2,1,0:T(8,128)(2,1)S(1)} %fusion.39), channel_id=5, replica_groups=mesh['groups'=2,'tm'=8,'space'=2] {'tm'}, dimensions={0}, use_global_device_ids=true | all-gather | bytes 20160 | tf_op jit(solution)/shard_map/all_gather | solution.py:41
  203.7 5.6 %while.27 = (s32[]{:T(128)}, f32[10,112,112]{2,1,0:T(8,128)S(1)}, f32[10,112]{1,0:T(8,128)S(1)}, s32[]{:T(128)}, bf16[8,10,112,112]{3,2,1,0:T(8,128)(2,1)}, /*in...) while((s32[]{:T(128)}, f32[10,112,112]{2,1,0:T(8,128)S(1)}, ...), condition=%wide.region_9.10_spmd, body=%wide.region_8.9_spmd.sunk | while | flops 253126 | bytes 1265763 | solution.py:56
  209.4 2.3 all_gather.46
  222.6 3.1 %select_convert_fusion = (bf16[1,4,32,2240]{3,2,1,0:T(8,128)(2,1)}, bf16[1,4,32,2240]{3,2,1,0:T(8,128)(2,1)}) fusion(bf16[1,4,32,2240]{3,2,1,0:T(8,128)(2,1)} %reshape.76, bf16[1,4,32,2240]{3,2,1,0:T(8,128)(2,1)} %param.10, bf16[1,4,32,2240]{3,2,1,0:T(8,128)(2,1)} %reshape.75, bf16[1,4,32,2240]{3,2,1,0:T(8,128)(2,1)} %param.9), kind=kLoop, calls=%fused_computation.59 | loop fusion | flops 2007040 | bytes 3440640 | tf_op jit(solution)/shard_map/convert_element_type | solution.py:151
  225.7 2.7 fusion.22
  228.4 46.1 %all-reduce.11.cloned.1.call-done = f32[3,3,2240]{2,1,0:T(4,128)} async-done(((f32[3,3,2240]{2,1,0:T(4,128)}), f32[3,3,2240]{2,1,0:T(4,128)}) %all-reduce.11.cloned.1.call-update) | async-done | bytes 80656 | tf_op jit(solution)/shard_map/psum | solution.py:164
  (180 shorter events, 53.2 us)
Async XLA Ops:
  7.2 16.2 %reduce-scatter.7.cloned.1.call-start = ((), (), s32[]{:S(2)}) async-start(), calls=%async_computation.2 | async-start | bytes 1720320 | tf_op jit(solution)/shard_map/reduce_scatter | solution.py:96
  13.2 10.3 %copy-start.3 = (bf16[1,4,32,2240]{3,2,1,0:T(8,128)(2,1)S(1)}, bf16[1,4,32,2240]{3,2,1,0:T(8,128)(2,1)}, u32[]{:S(2)}) copy-start(bf16[1,4,32,2240]{3,2,1,0:T(8,128)(2,1)} %param.10) | copy-start | bytes 1720324
  13.2 15.4 %copy-start.11 = (bf16[1,4,32,2240]{3,2,1,0:T(8,128)(2,1)S(1)}, bf16[1,4,32,2240]{3,2,1,0:T(8,128)(2,1)}, u32[]{:S(2)}) copy-start(bf16[1,4,32,2240]{3,2,1,0:T(8,128)(2,1)} %param.9) | copy-start | bytes 1720324
  13.2 91.0 %all-gather.11.cloned.1.call-start = ((), (), s32[]{:S(2)}) async-start(), calls=%async_computation.6 | async-start | bytes 5160960 | tf_op jit(solution)/shard_map/all_gather | solution.py:25
  23.4 5.3 %copy-start.1 = (bf16[1,4,32,2240]{3,2,1,0:T(8,128)(2,1)S(1)}, bf16[1,4,32,2240]{3,2,1,0:T(8,128)(2,1)}, u32[]{:S(2)}) copy-start(bf16[1,4,32,2240]{3,2,1,0:T(8,128)(2,1)} %param.12) | copy-start | bytes 1720324
  23.4 103.3 %reduce-scatter.9.cloned.1.call-start = ((), (), s32[]{:S(2)}) async-start(), calls=%async_computation.3 | async-start | bytes 1720320 | tf_op jit(solution)/shard_map/reduce_scatter | solution.py:124
  26.4 9.1 %collective-permute-start.4 = (f32[6,112]{1,0:T(8,128)S(1)}, f32[6,112]{1,0:T(8,128)S(1)}, u32[]{:S(2)}, u32[]{:S(2)}) collective-permute-start(f32[6,112]{1,0:T(8,128)S(1)} %slice.158), channel_id=1, source_target_pairs={{0,1},{2,3},{4,5},{6,7},{8,9},{10,11},{12,13},{14,15},{16,17},{18,... | collective-permute-start | bytes 8072
  35.5 73.7 %copy-start.8 = (bf16[128,20,112]{0,2,1:T(8,128)(2,1)}, bf16[128,20,112]{0,2,1:T(8,128)(2,1)S(1)}, u32[]{:S(2)}) copy-start(bf16[128,20,112]{0,2,1:T(8,128)(2,1)S(1)} %copy.40) | copy-start | bytes 1720324
  109.1 3.7 %copy-start.28 = (f32[20,1,128]{2,1,0:T(1,128)}, f32[20,1,128]{2,1,0:T(1,128)S(1)}, u32[]{:S(2)}) copy-start(f32[20,1,128]{2,1,0:T(1,128)S(1)} %fusion.44) | copy-start | bytes 30724
  109.2 3.6 %copy-start.35 = (f32[128,20]{0,1:T(8,128)}, f32[128,20]{0,1:T(8,128)S(1)}, u32[]{:S(2)}) copy-start(f32[128,20]{0,1:T(8,128)S(1)} %fusion.34) | copy-start | bytes 30724
  112.8 35.8 %all-reduce.9.cloned.1.call-start = ((), (), s32[]{:S(2)}) async-start(), calls=%async_computation.4 | async-start | bytes 221184 | tf_op jit(solution)/shard_map/psum | solution.py:164
  112.9 4.4 %collective-permute-start.1 = (bf16[1,1,32,2240]{3,2,1,0:T(8,128)(2,1)S(1)}, bf16[1,1,32,2240]{3,2,1,0:T(8,128)(2,1)S(1)}, u32[]{:S(2)}, u32[]{:S(2)}) collective-permute-start(bf16[1,1,32,2240]{3,2,1,0:T(8,128)(2,1)S(1)} %get-tuple-element.172), channel_id=1, source_target_pairs={{1,0},{3,2},{5,4},{7,6},{9,8},{11,10},{13,12},{15,14},{17,16},{19,... | collective-permute-start | bytes 430088 | tf_op jit(solution)/shard_map/ppermute | solution.py:18
  114.2 4.0 %collective-permute-start = (bf16[1,1,32,2240]{3,2,1,0:T(8,128)(2,1)S(1)}, bf16[1,1,32,2240]{3,2,1,0:T(8,128)(2,1)S(1)}, u32[]{:S(2)}, u32[]{:S(2)}) collective-permute-start(bf16[1,1,32,2240]{3,2,1,0:T(8,128)(2,1)S(1)} %get-tuple-element.171), channel_id=1, source_target_pairs={{0,1},{2,3},{4,5},{6,7},{8,9},{10,11},{12,13},{14,15},{16,17},{18,... | collective-permute-start | bytes 430088 | tf_op jit(solution)/shard_map/ppermute | solution.py:15
  119.8 13.9 %copy-start.29 = (f32[3,3,2240]{2,1,0:T(4,128)S(1)}, f32[3,3,2240]{2,1,0:T(4,128)}, u32[]{:S(2)}) copy-start(f32[3,3,2240]{2,1,0:T(4,128)} %param.13) | copy-start | bytes 241924
  120.7 83.0 %all-gather.13.cloned.1.call-start = ((), (), s32[]{:S(2)}) async-start(), calls=%async_computation.7 | async-start | bytes 2580480 | tf_op jit(solution)/shard_map/all_gather | solution.py:41
  128.6 146.0 %all-reduce.11.cloned.1.call-start = ((), (), s32[]{:S(2)}) async-start(), calls=%async_computation.5 | async-start | bytes 221184 | tf_op jit(solution)/shard_map/psum | solution.py:164
  128.7 5.8 %collective-permute-start.3 = (bf16[1,1,32,2240]{3,2,1,0:T(8,128)(2,1)S(1)}, bf16[1,1,32,2240]{3,2,1,0:T(8,128)(2,1)S(1)}, u32[]{:S(2)}, u32[]{:S(2)}) collective-permute-start(bf16[1,1,32,2240]{3,2,1,0:T(8,128)(2,1)S(1)} %get-tuple-element.170), channel_id=1, source_target_pairs={{1,0},{3,2},{5,4},{7,6},{9,8},{11,10},{13,12},{15,14},{17,16},{19,... | collective-permute-start | bytes 430088 | tf_op jit(solution)/shard_map/ppermute | solution.py:18
  130.0 5.2 %collective-permute-start.2 = (bf16[1,1,32,2240]{3,2,1,0:T(8,128)(2,1)S(1)}, bf16[1,1,32,2240]{3,2,1,0:T(8,128)(2,1)}, u32[]{:S(2)}, u32[]{:S(2)}) collective-permute-start(bf16[1,1,32,2240]{3,2,1,0:T(8,128)(2,1)S(1)} %get-tuple-element.169), channel_id=1, source_target_pairs={{0,1},{2,3},{4,5},{6,7},{8,9},{10,11},{12,13},{14,15},{16,17},{18,... | collective-permute-start | bytes 430088 | tf_op jit(solution)/shard_map/ppermute | solution.py:15
  149.3 4.1 %copy-start.36 = (f32[128,20]{0,1:T(8,128)S(1)}, f32[128,20]{0,1:T(8,128)}, u32[]{:S(2)}) copy-start(f32[128,20]{0,1:T(8,128)} %copy-done.35) | copy-start | bytes 30724
  159.0 9.4 %copy-start.20 = (f32[2240]{0:T(1024)S(1)}, f32[2240]{0:T(1024)}, u32[]{:S(2)}) copy-start(f32[2240]{0:T(1024)} %get-tuple-element.137) | copy-start | bytes 26884
  166.3 5.6 %copy-start.30 = (f32[16,112]{1,0:T(8,128)}, f32[16,112]{1,0:T(8,128)S(1)}, u32[]{:S(2)}) copy-start(f32[16,112]{1,0:T(8,128)S(1)} %fusion.1) | copy-start | bytes 21508
  166.3 8.9 %collective-permute-start.5 = (f32[6,112]{1,0:T(8,128)S(1)}, f32[6,112]{1,0:T(8,128)S(1)}, u32[]{:S(2)}, u32[]{:S(2)}) collective-permute-start(f32[6,112]{1,0:T(8,128)S(1)} %slice.159), channel_id=1, source_target_pairs={{0,1},{2,3},{4,5},{6,7},{8,9},{10,11},{12,13},{14,15},{16,17},{18,... | collective-permute-start | bytes 8072
  203.7 5.6 %copy-start.12 = (f32[10,112,112]{2,1,0:T(8,128)S(1)}, f32[10,112,112]{2,1,0:T(8,128)}, u32[]{:S(2)}) copy-start(f32[10,112,112]{2,1,0:T(8,128)} %reduce-scatter.9.cloned.1.call-done) | copy-start | bytes 1505284
  209.3 4.4 %copy-start.5 = (bf16[128,20,112]{0,2,1:T(8,128)(2,1)S(1)}, bf16[128,20,112]{0,2,1:T(8,128)(2,1)}, u32[]{:S(2)}) copy-start(bf16[128,20,112]{0,2,1:T(8,128)(2,1)} %copy-done.4) | copy-start | bytes 1720324
  (27 other events, 70.3 us)
Sparse Core Ops, SparseCore 0:
  13.4 9.9 reduce-scatter.6
  25.6 78.6 all-gather.10
  113.0 13.7 reduce-scatter.8
  129.5 19.0 all-reduce.8
  150.7 52.2 all-gather.12
  206.2 68.3 all-reduce.10
